TPU v7x, 512 devices: a whole 4x8x8 slice. The times are simulated.
512 devices in a mesh: ent: 128 (over y, z, core), rep: 4 (over x).
Axes of the slice: x: 4, y: 8, z: 8, core: 2. Of those that a mesh axis runs over, the one named last changes fastest.
Arguments:
- item_factors: bfloat16 [524288, 128], P(('ent', 'rep')), may hold values from -0.1 to 0.1
- tile_items: int32 [128, 4, 256, 32], P('ent', 'rep'), may hold values from 0 to 1023
- send_tiles: int32 [128, 4, 128], P('ent', 'rep'), may hold values from 1 to 2, as said below
- tile_users: int32 [128, 4, 256, 1], P('ent', 'rep'), may hold values from 0 to 7
- tile_counts: int32 [128, 4, 256, 32], P('ent', 'rep'), may hold values from 0 to 31
- recv_tiles: int32 [128, 4, 128], P('ent', 'rep'), may hold values from 1 to 2, as said below
Outputs:
- user_factors: float32 [1024, 128], P(('ent', 'rep'))
- item_rhs: float32 [524288, 128], P(('ent', 'rep'))
Inputs may be any that keep to these rules, and one draw needn't show every extreme that they name: send_tiles[e, r, p] counts the leading tile slots p * 2 to p * 2 + 1 of device (e, r) that are live; every device sends 2 tiles to some peer and receives 2 tiles from some peer. recv_tiles[p, r, e] equals send_tiles[e, r, p].
All inputs are finite; a program needn't handle non-finite values.
Results may differ from a plain program's by a relative error of at most 0.0009.
The roundings to bfloat16 on the way count: a program that leaves them out, or rounds other values in their place, can miss the bound.
Values may be sent and summed in bfloat16 or wider, within the bound.
A program may use at most 64 MiB of HBM per device.

v0:
```python
import jax
import jax.numpy as jnp
from jax import lax
from jax.sharding import PartitionSpec as P

U_DEV = 2
ALPHA = 40.0
RIDGE = 1.0
RHS_SCALE = 1.0 / 640.0


def solve_users(gram, rhs):
    lower = jnp.linalg.cholesky(gram)
    halfway = lax.linalg.triangular_solve(lower, rhs[..., None], left_side=True, lower=True)
    result = lax.linalg.triangular_solve(
        lower, halfway, left_side=True, lower=True, transpose_a=True
    )
    return result[..., 0]


def shards(item_factors, tile_items, send_tiles, tile_users, tile_counts, recv_tiles):
    highest = lax.Precision.HIGHEST
    rank_width = item_factors.shape[1]
    item_count = item_factors.shape[0]
    n_ent = lax.axis_size("ent")
    tile_slots = tile_items.shape[2]
    tile_rows = tile_items.shape[3]
    seg_count = tile_users.shape[3]
    seg_length = tile_rows // seg_count
    slot_cap = tile_slots // n_ent
    user_block = U_DEV * lax.axis_size("rep")
    item_ids = tile_items.reshape(tile_slots, tile_rows)
    slot_pos = jnp.arange(tile_slots, dtype=jnp.int32) % slot_cap
    live_send = slot_pos < jnp.repeat(send_tiles.reshape(n_ent), slot_cap)
    live_recv = slot_pos < jnp.repeat(recv_tiles.reshape(n_ent), slot_cap)
    partial_gram = lax.dot_general(
        item_factors, item_factors, (((0,), (0,)), ((), ())), preferred_element_type=jnp.float32
    )
    picked = jnp.take(item_factors, item_ids.reshape(-1), axis=0).reshape(
        tile_slots, tile_rows, rank_width
    )
    picked = jnp.where(live_send[:, None, None], picked, jnp.zeros((), jnp.bfloat16))
    incoming = lax.all_to_all(
        picked.reshape(n_ent, slot_cap * tile_rows, rank_width),
        "ent",
        split_axis=0,
        concat_axis=0,
        tiled=True,
    )
    counts_int = tile_counts.reshape(tile_slots, tile_rows)
    counts_f = counts_int.astype(jnp.float32)
    gram_weight = ALPHA * counts_f
    rhs_weight = jnp.where(
        live_recv[:, None] & (counts_int > 0), 1.0 + ALPHA * counts_f, jnp.float32(0.0)
    )
    owners = tile_users.reshape(tile_slots * seg_count)
    selector = owners[None, :] == jnp.arange(user_block, dtype=jnp.int32)[:, None]
    selector_f = selector.astype(jnp.float32)
    src_group = 1
    while (
        src_group * 2 <= n_ent
        and n_ent % (src_group * 2) == 0
        and (src_group * 2 * slot_cap * tile_rows <= 4096)
    ):
        src_group = src_group * 2
    tiles_blk = src_group * slot_cap
    block_count = tile_slots // tiles_blk
    runs_blk = tiles_blk * seg_count

    def accumulate(state_pair, pieces):
        gram_run, rhs_run = state_pair
        rows_blk, gram_blk, rhs_blk, select_blk = pieces
        weighted = (gram_blk[:, :, None] * rows_blk).astype(jnp.bfloat16)
        rows_seg = rows_blk.reshape(tiles_blk, seg_count, seg_length, rank_width)
        weighted = weighted.reshape(tiles_blk, seg_count, seg_length, rank_width)
        run_gram = jnp.einsum(
            "tsri,tsrj->tsij", weighted, rows_seg, preferred_element_type=jnp.float32
        )
        run_gram = run_gram.reshape(runs_blk, rank_width * rank_width)
        run_rhs = jnp.einsum(
            "tsr,tsri->tsi",
            rhs_blk.reshape(tiles_blk, seg_count, seg_length),
            rows_seg.astype(jnp.float32),
            precision=highest,
        )
        run_rhs = run_rhs.reshape(runs_blk, rank_width)
        gram_run = gram_run + jnp.dot(select_blk, run_gram, precision=highest)
        rhs_run = rhs_run + jnp.dot(select_blk, run_rhs, precision=highest)
        return ((gram_run, rhs_run), None)

    block_pieces = (
        incoming.reshape(block_count, tiles_blk, tile_rows, rank_width),
        gram_weight.reshape(block_count, tiles_blk, tile_rows),
        rhs_weight.reshape(block_count, tiles_blk, tile_rows),
        jnp.transpose(selector_f.reshape(user_block, block_count, runs_blk), (1, 0, 2)),
    )
    start_pair = (
        jnp.zeros((user_block, rank_width * rank_width), jnp.float32),
        jnp.zeros((user_block, rank_width), jnp.float32),
    )
    (gram_acc, rhs_acc), _ = lax.scan(accumulate, start_pair, block_pieces)
    identity_mat = jnp.eye(rank_width, dtype=jnp.float32)
    added_term = lax.psum(partial_gram, ("ent", "rep")) + RIDGE * identity_mat
    own_gram, own_rhs = (
        lax.psum_scatter(gram_acc, "rep", scatter_dimension=0, tiled=True),
        lax.psum_scatter(rhs_acc, "rep", scatter_dimension=0, tiled=True),
    )
    own_factors = solve_users(own_gram.reshape(-1, rank_width, rank_width) + added_term, own_rhs)
    solved = lax.all_gather(own_factors.astype(jnp.bfloat16), "rep", axis=0, tiled=True)
    run_factor = lax.dot_general(
        selector.astype(jnp.bfloat16),
        solved,
        (((0,), (0,)), ((), ())),
        preferred_element_type=jnp.float32,
    )
    back_factor, back_weight = (
        lax.all_to_all(
            run_factor.reshape(n_ent, slot_cap, seg_count * rank_width),
            "ent",
            split_axis=0,
            concat_axis=0,
            tiled=True,
        ),
        lax.all_to_all(
            rhs_weight.reshape(n_ent, slot_cap, tile_rows),
            "ent",
            split_axis=0,
            concat_axis=0,
            tiled=True,
        ),
    )

    def spread(running, pieces):
        factor_blk, weight_blk, item_blk = pieces
        contrib = (weight_blk[:, :, :, None] * factor_blk[:, :, None, :]).reshape(-1, rank_width)
        return (
            running + jax.ops.segment_sum(contrib, item_blk.reshape(-1), num_segments=item_count),
            None,
        )

    spread_pieces = (
        back_factor.reshape(block_count, tiles_blk, seg_count, rank_width),
        back_weight.reshape(block_count, tiles_blk, seg_count, seg_length),
        item_ids.reshape(block_count, tiles_blk, tile_rows),
    )
    item_rhs, _ = lax.scan(spread, jnp.zeros((item_count, rank_width), jnp.float32), spread_pieces)
    return (own_factors, item_rhs * RHS_SCALE)


def solution(mesh):
    in_specs = (
        P(("ent", "rep"), None),
        P("ent", "rep", None, None),
        P("ent", "rep", None),
        P("ent", "rep", None, None),
        P("ent", "rep", None, None),
        P("ent", "rep", None),
    )
    out_specs = (P(("ent", "rep"), None), P(("ent", "rep"), None))
    return jax.shard_map(shards, mesh=mesh, in_specs=in_specs, out_specs=out_specs, check_vma=False)
```

profile of v0, /device:TPU:1, one launch (start us, length us, event | category | flops | bytes accessed | tf_op | source)
XLA Modules:
  0.0 525.8 jit_solution(16828590585126697929)
XLA Ops:
  7.2 0.9 copy.43
  8.1 0.1 reshape_reshape.9
  8.4 0.7 broadcast_compare_fusion.2
  9.1 0.1 copy.42
  9.2 24.0 %gather_fusion = bf16[8192,128]{1,0:T(8,128)(2,1)S(1)} fusion(bf16[1024,128]{1,0:T(8,128)(2,1)S(1)} %copy-done, s32[8192]{0:T(1024)S(1)} %broadcast_clamp_fusion), kind=kCustom, calls=%fused_computation | custom fusion | bytes 4227072 | tf_op jit(solution)/shard_map/jit(_take)/gather | solution.py:39
  33.2 4.6 select_select_fusion
  37.8 18.6 %all-to-all-start = ((bf16[128,64,128]{2,1,0:T(8,128)(2,1)}), bf16[128,64,128]{2,1,0:T(8,128)(2,1)S(1)}, u32[]{:S(2)}, u32[]{:S(2)}) async-start(bf16[128,64,128]{2,1,0:T(8,128)(2,1)} %select_select_fusion), calls=%async_computation | async-start | bytes 4194304 | tf_op jit(solution)/shard_map/all_to_all | solution.py:43
  56.4 0.9 fusion.25
  57.4 0.5 broadcast.218
  57.9 0.7 reduce.9
  58.7 0.1 broadcast_in_dim.73
  59.0 0.1 copy.45
  59.3 0.1 copy.50
  59.4 1.3 dynamic-slice
  61.4 0.1 add_select_fusion
  61.5 0.9 and_select_fusion
  62.4 46.3 %all-to-all-done = bf16[128,64,128]{2,1,0:T(8,128)(2,1)S(1)} async-done(((bf16[128,64,128]{2,1,0:T(8,128)(2,1)}), bf16[128,64,128]{2,1,0:T(8,128)(2,1)S(1)}, u32[]{:S(2)}, u32[]{:S(2)}) %all-to-all-start) | async-done | bytes 2097184 | tf_op jit(solution)/shard_map/all_to_all | solution.py:43
  108.7 7.6 %all-to-all-start.1 = ((f32[128,2,32]{2,1,0:T(2,128)}), f32[128,2,32]{2,1,0:T(2,128)S(1)}, u32[]{:S(2)}, u32[]{:S(2)}) async-start(f32[128,2,32]{2,1,0:T(2,128)} %and_select_fusion), calls=%async_computation.1 | async-start | bytes 262144 | tf_op jit(solution)/shard_map/all_to_all | solution.py:124
  116.3 0.2 all-reduce.7.cloned.1.call-start
  116.5 37.8 %while.24 = (s32[]{:T(128)}, f32[8,16384]{1,0:T(8,128)S(1)}, f32[8,128]{1,0:T(8,128)S(1)}, f32[2,8,128]{2,1,0:T(8,128)S(1)}, f32[2,128,32]{2,1,0:T(8,128)S(1)}, ...) while((s32[]{:T(128)}, f32[8,16384]{1,0:T(8,128)S(1)}, ...), condition=%wide.region_1.2_spmd.clone, body=%wide.region_0.1_spmd.clone.sunk | while | flops 345245696 | bytes 21267580 | solution.py:101
  116.5 5.2 fusion.49
  121.7 12.5 %convolution_add_fusion.4 = f32[8,16384]{1,0:T(8,128)S(1)} fusion(f32[16,8,128,128]{3,2,1,0:T(8,128)} %bitcast.121, f32[8,16384]{1,0:T(8,128)S(1)} %get-tuple-element.219, pred[]{:T(512)S(6)} %compare.15, f32[2,8,128]{2,1,0:T(8,128)S(1)} %get-tuple-element.230, s32[]{:T(128)} %get-tuple-element.218), kind=kOutput, calls=%fused_computation.6.clone.1 | convolution fusion | flops 201588736 | bytes 9441285 | tf_op jit(solution)/shard_map/while/body/eval_jaxpr/dot_general | solution.py:87
  134.3 0.9 fusion.50
  135.2 0.2 convolution_add_fusion.5
  135.4 5.2 fusion.49
  140.6 12.5 %convolution_add_fusion.4 = f32[8,16384]{1,0:T(8,128)S(1)} fusion(f32[16,8,128,128]{3,2,1,0:T(8,128)} %bitcast.121, f32[8,16384]{1,0:T(8,128)S(1)} %get-tuple-element.219, pred[]{:T(512)S(6)} %compare.15, f32[2,8,128]{2,1,0:T(8,128)S(1)} %get-tuple-element.230, s32[]{:T(128)} %get-tuple-element.218), kind=kOutput, calls=%fused_computation.6.clone.1 | convolution fusion | flops 201588736 | bytes 9441285 | tf_op jit(solution)/shard_map/while/body/eval_jaxpr/dot_general | solution.py:87
  153.2 0.9 fusion.50
  154.1 0.2 convolution_add_fusion.5
  154.3 0.8 copy-done.1
  155.2 186.7 %all-reduce.5.cloned.1.call-done = f32[128,128]{1,0:T(8,128)} async-done(((f32[128,128]{1,0:T(8,128)}), f32[128,128]{1,0:T(8,128)}) %all-reduce.5.cloned.1.call-update) | async-done | bytes 65552 | tf_op jit(solution)/shard_map/psum | solution.py:103
  341.9 0.9 convert_add_fusion
  342.9 8.1 %all-reduce.1 = f32[8,128]{1,0:T(8,128)S(1)} all-reduce(f32[8,128]{1,0:T(8,128)S(1)} %get-tuple-element.68), channel_id=3, replica_groups=mesh['ent'=128,'rep'=4] {'rep'}, use_global_device_ids=true, to_apply=%region_6.7.clone | all-reduce | flops 1024 | bytes 8192
  350.9 37.3 %all-reduce.7.cloned.1.call-done = f32[8,16384]{1,0:T(8,128)} async-done(((f32[8,16384]{1,0:T(8,128)}), f32[8,16384]{1,0:T(8,128)}) %all-reduce.7.cloned.1.call-update) | async-done | bytes 524304
  388.3 1.1 dynamic-slice_bitcast_fusion.2
  389.6 23.5 %custom-call.9 = f32[2,128,128]{2,1,0:T(8,128)S(1)} custom-call(f32[2,128,128]{2,1,0:T(8,128)S(1)} %fusion.20), custom_call_target="Cholesky" | custom-call | tf_op jit(solution)/shard_map/jit(cholesky)/cholesky | solution.py:13
  413.1 0.1 compare_reduce_fusion
  413.3 19.7 %custom-call.10 = f32[2,1,128,128]{2,3,1,0:T(8,128)S(1)} custom-call(f32[2,1,128,128]{3,2,1,0:T(8,128)S(1)} %select_bitcast_fusion), custom_call_target="InvertDiagBlocksLowerTriangular" | custom-call | tf_op jit(solution)/shard_map/triangular_solve | solution.py:15
  433.0 0.2 convolution_bitcast_fusion
  433.3 0.3 fusion.17
  433.6 6.8 %all-gather = bf16[4,2,128]{2,1,0:T(2,128)(2,1)S(1)} all-gather(bf16[1,2,128]{2,1,0:T(2,128)(2,1)S(1)} %convert_bitcast_fusion), channel_id=1, replica_groups=mesh['ent'=128,'rep'=4] {'rep'}, dimensions={0}, use_global_device_ids=true | all-gather | bytes 2560 | tf_op jit(solution)/shard_map/all_gather | solution.py:109
  440.4 0.2 fusion.22
  440.6 30.5 %all_to_all.15 = f32[128,2,128]{2,1,0:T(2,128)S(1)} all-to-all(f32[128,2,128]{2,1,0:T(2,128)S(1)} %bitcast.132), channel_id=1, replica_groups=mesh['ent'=128,'rep'=4] {'ent'}, dimensions={0} | all-to-all | bytes 262144 | tf_op jit(solution)/shard_map/all_to_all | solution.py:117
  471.2 46.8 %while.23 = (s32[]{:T(128)}, f32[1024,128]{1,0:T(8,128)S(1)}, s32[2,128,32]{2,1,0:T(8,128)S(1)}, f32[2,128,1,32]{3,1,2,0:T(8,128)S(1)}, f32[2,128,1,128]{3,1,2,0:T(8,128)S(1)}, /*index=5*/s32[]{:T(128)}) while((s32[]{:T(128)}, f32[1024,128]{1,0:T(8,128)S(1)}, s32[2,128,32]{2,1,0:T(8,128)S(1)}, f32[2,128,1,32]{3,1,2,0:T(8,128)S(1)}, ...), condition=%wide.region_9.10_spmd, body=%wide.region_7.9_spmd.sunk | while | flops 1048578 | bytes 8749137 | solution.py:146
  471.4 0.6 bitcast_multiply_fusion.2
  472.1 22.6 %scatter_fusion = f32[1024,128]{1,0:T(8,128)S(1)} fusion(f32[1024,128]{1,0:T(8,128)S(1)} %get-tuple-element.243, s32[4096]{0:T(1024)S(1)} %reshape.259, f32[4096,128]{1,0:T(8,128)S(1)} %bitcast_multiply_fusion.2), kind=kCustom, calls=%fused_computation.1.clone.1 | custom fusion | flops 524288 | bytes 6307840 | tf_op jit(solution)/shard_map/while/body/eval_jaxpr/scatter-add | solution.py:137
  494.8 0.6 bitcast_multiply_fusion.2
  495.5 22.6 %scatter_fusion = f32[1024,128]{1,0:T(8,128)S(1)} fusion(f32[1024,128]{1,0:T(8,128)S(1)} %get-tuple-element.243, s32[4096]{0:T(1024)S(1)} %reshape.259, f32[4096,128]{1,0:T(8,128)S(1)} %bitcast_multiply_fusion.2), kind=kCustom, calls=%fused_computation.1.clone.1 | custom fusion | flops 524288 | bytes 6307840 | tf_op jit(solution)/shard_map/while/body/eval_jaxpr/scatter-add | solution.py:137
  518.1 0.8 broadcast_multiply_fusion
  (59 shorter events, 1.7 us)
Async XLA Ops:
  7.2 2.0 copy-start
  37.8 20.1 %copy-start.5 = (s32[1,1,128]{2,1,0:T(1,128)S(1)}, s32[1,1,128]{2,1,0:T(1,128)}, u32[]{:S(2)}) copy-start(s32[1,1,128]{2,1,0:T(1,128)} %param.15) | copy-start | bytes 1540
  37.8 21.0 %copy-start.2 = (s32[1,1,256,32]{2,3,1,0:T(8,128)S(1)}, s32[1,1,256,32]{2,3,1,0:T(8,128)}, u32[]{:S(2)}) copy-start(s32[1,1,256,32]{2,3,1,0:T(8,128)} %param.14) | copy-start | bytes 98308
  37.8 23.6 %copy-start.3 = (s32[1,1,256,1]{2,3,1,0:T(1,128)S(1)}, s32[1,1,256,1]{2,3,1,0:T(1,128)}, u32[]{:S(2)}) copy-start(s32[1,1,256,1]{2,3,1,0:T(1,128)} %param.13) | copy-start | bytes 3076
  37.8 70.9 %all-to-all-start = ((bf16[128,64,128]{2,1,0:T(8,128)(2,1)}), bf16[128,64,128]{2,1,0:T(8,128)(2,1)S(1)}, u32[]{:S(2)}, u32[]{:S(2)}) async-start(bf16[128,64,128]{2,1,0:T(8,128)(2,1)} %select_select_fusion), calls=%async_computation | async-start | bytes 4194304 | tf_op jit(solution)/shard_map/all_to_all | solution.py:43
  56.4 285.5 %all-reduce.5.cloned.1.call-start = ((), (), s32[]{:S(2)}) async-start(), calls=%async_computation.3 | async-start | bytes 131072 | tf_op jit(solution)/shard_map/psum | solution.py:103
  108.7 332.0 %all-to-all-start.1 = ((f32[128,2,32]{2,1,0:T(2,128)}), f32[128,2,32]{2,1,0:T(2,128)S(1)}, u32[]{:S(2)}, u32[]{:S(2)}) async-start(f32[128,2,32]{2,1,0:T(2,128)} %and_select_fusion), calls=%async_computation.1 | async-start | bytes 262144 | tf_op jit(solution)/shard_map/all_to_all | solution.py:124
  116.3 272.0 %all-reduce.7.cloned.1.call-start = ((), (), s32[]{:S(2)}) async-start(), calls=%async_computation.4 | async-start | bytes 1048576
  154.3 0.8 copy-start.1
  433.6 37.7 %copy-start.4 = (f32[2,1,128]{2,1,0:T(1,128)}, f32[2,1,128]{2,1,0:T(1,128)S(1)}, u32[]{:S(2)}) copy-start(f32[2,1,128]{2,1,0:T(1,128)S(1)} %fusion.17) | copy-start | bytes 3076
Sparse Core Ops, SparseCore 0:
  62.2 279.6 all-reduce.4
  344.9 43.2 all-reduce.6
where the time goes:
time: 526 us
  waiting for transfers between devices  270 us (51%)
  other arithmetic  98.5 us (19%)
  blocking collectives  45.4 us (9%)
  matrix products  39.3 us (7%)
  local copies, waits for them, and re-layouts  30.6 us (6%)
  starting transfers between devices  26.4 us (5%)
  between operations  15 us (3%)
    psum x1, waiting for transfers between devices, shards(): added_term = lax.psum(partial_gram, ('ent', 'rep')) + RIDGE * identity_mat  187 us
    all_to_all x1, waiting for transfers between devices, shards(): lax.all_to_all(picked.reshape(n_ent, slot_cap * tile_rows, rank_width), '...  46.3 us
    scatter-add x2, other arithmetic, spread(): jax.ops.segment_sum(contrib, item_blk.reshape(-1), num_segments=item_count)  45.1 us
    unnamed x3, waiting for transfers between devices  37.4 us
    all_to_all x1, blocking collectives, shards(): lax.all_to_all(run_factor.reshape(n_ent, slot_cap, seg_count * rank_width...  30.5 us
    dot_general x2, matrix products, accumulate(): gram_run = gram_run + jnp.dot(select_blk, run_gram, precision=highest)  25 us
    gather x1, local copies, waits for them, and re-layouts, shards(): jnp.take(item_factors, item_ids.reshape(-1), axis=0)  24 us
    another operation x4, other arithmetic, solve_users(): lower = jnp.linalg.cholesky(gram)  23.6 us
  transfers between devices with their start and end apart: 4, of which 3 were waited for; matrix products, arithmetic and copies ran while one was open for 17% of the time, Pallas kernels for 0%

commit v1 on v0

--- a/solution.py
+++ b/solution.py
@@ -100,7 +100,7 @@
     )
     (gram_acc, rhs_acc), _ = lax.scan(accumulate, start_pair, block_pieces)
     identity_mat = jnp.eye(rank_width, dtype=jnp.float32)
-    added_term = lax.psum(partial_gram, ("ent", "rep")) + RIDGE * identity_mat
+    added_term = lax.psum(lax.psum(partial_gram, "ent"), "rep") + RIDGE * identity_mat
     own_gram, own_rhs = (
         lax.psum_scatter(gram_acc, "rep", scatter_dimension=0, tiled=True),
         lax.psum_scatter(rhs_acc, "rep", scatter_dimension=0, tiled=True),

time: 526 us -> 448 us (0.85)
  waiting for transfers between devices: 270 us -> 194 us
    psum x1, waiting for transfers between devices: 187 us -> 115 us  [shards(): lax.psum(partial_gram, 'ent')]
    unnamed x3, waiting for transfers between devices: 37.4 us -> 29.6 us
  transfers between devices with their start and end apart: 4 -> 4, of which waited for: 3 -> 3; matrix products, arithmetic and copies ran while one was open for 17% -> 20% of each run, Pallas kernels for 0% -> 0%
where the time goes in v1:
time: 448 us; the launch traced here: 447 us
  waiting for transfers between devices  194 us (43%)
  other arithmetic  98.5 us (22%)
  blocking collectives  46.3 us (10%)
  matrix products  39.2 us (9%)
  local copies, waits for them, and re-layouts  29.8 us (7%)
  starting transfers between devices  24.6 us (5%)
  between operations  15 us (3%)
    psum x1, waiting for transfers between devices, shards(): lax.psum(partial_gram, 'ent')  115 us
    all_to_all x1, waiting for transfers between devices, shards(): lax.all_to_all(picked.reshape(n_ent, slot_cap * tile_rows, rank_width), '...  49.3 us
    scatter-add x2, other arithmetic, spread(): jax.ops.segment_sum(contrib, item_blk.reshape(-1), num_segments=item_count)  45.1 us
    all_to_all x1, blocking collectives, shards(): lax.all_to_all(run_factor.reshape(n_ent, slot_cap, seg_count * rank_width...  30.6 us
    unnamed x3, waiting for transfers between devices  29.6 us
    dot_general x2, matrix products, accumulate(): gram_run = gram_run + jnp.dot(select_blk, run_gram, precision=highest)  25 us
    gather x1, local copies, waits for them, and re-layouts, shards(): jnp.take(item_factors, item_ids.reshape(-1), axis=0)  24 us
    another operation x4, other arithmetic, solve_users(): lower = jnp.linalg.cholesky(gram)  23.6 us
  transfers between devices with their start and end apart: 4, of which 3 were waited for; matrix products, arithmetic and copies ran while one was open for 20% of the time, Pallas kernels for 0%

profile of v1, /device:TPU:1, one launch (start us, length us, event | category | flops | bytes accessed | tf_op | source)
XLA Modules:
  0.0 447.2 jit_solution(2884424658412365584)
XLA Ops:
  7.2 0.9 copy.43
  8.1 0.1 reshape_reshape.9
  8.4 0.7 broadcast_compare_fusion.2
  9.1 0.1 copy.42
  9.2 24.0 %gather_fusion = bf16[8192,128]{1,0:T(8,128)(2,1)S(1)} fusion(bf16[1024,128]{1,0:T(8,128)(2,1)S(1)} %copy-done, s32[8192]{0:T(1024)S(1)} %broadcast_clamp_fusion), kind=kCustom, calls=%fused_computation | custom fusion | bytes 4227072 | tf_op jit(solution)/shard_map/jit(_take)/gather | solution.py:39
  33.2 4.6 %select_select_fusion = bf16[128,64,128]{2,1,0:T(8,128)(2,1)} fusion(bf16[128,64,128]{2,1,0:T(8,128)(2,1)S(1)} %bitcast.123, pred[128,64]{1,0:T(8,128)(4,1)S(1)} %compare_and_fusion, pred[128,64]{1,0:T(8,128)(4,1)S(1)} %copy.42), kind=kLoop, calls=%fused_computation.28 | loop fusion | flops 2097152 | bytes 4210688 | tf_op jit(solution)/shard_map/jit(_where)/select_n | solution.py:42
  37.8 18.6 %all-to-all-start = ((bf16[128,64,128]{2,1,0:T(8,128)(2,1)}), bf16[128,64,128]{2,1,0:T(8,128)(2,1)S(1)}, u32[]{:S(2)}, u32[]{:S(2)}) async-start(bf16[128,64,128]{2,1,0:T(8,128)(2,1)} %select_select_fusion), calls=%async_computation | async-start | bytes 4194304 | tf_op jit(solution)/shard_map/all_to_all | solution.py:43
  56.4 0.9 fusion.25
  57.4 0.5 broadcast.218
  57.9 0.7 reduce.9
  58.7 0.1 broadcast_in_dim.73
  58.9 0.1 copy.41
  59.0 0.1 copy.45
  59.2 0.1 add_select_fusion
  59.3 49.3 %all-to-all-done = bf16[128,64,128]{2,1,0:T(8,128)(2,1)S(1)} async-done(((bf16[128,64,128]{2,1,0:T(8,128)(2,1)}), bf16[128,64,128]{2,1,0:T(8,128)(2,1)S(1)}, u32[]{:S(2)}, u32[]{:S(2)}) %all-to-all-start) | async-done | bytes 2097184 | tf_op jit(solution)/shard_map/all_to_all | solution.py:43
  108.6 37.7 %while.24 = (s32[]{:T(128)}, f32[8,16384]{1,0:T(8,128)S(1)}, f32[8,128]{1,0:T(8,128)S(1)}, f32[2,8,128]{2,1,0:T(8,128)S(1)}, f32[2,128,32]{2,1,0:T(8,128)S(1)}, ...) while((s32[]{:T(128)}, f32[8,16384]{1,0:T(8,128)S(1)}, ...), condition=%wide.region_1.2_spmd.clone, body=%wide.region_0.1_spmd.clone.sunk | while | flops 345245696 | bytes 21267580 | solution.py:101
  108.7 5.2 %fusion.49 = f32[128,128,128]{2,1,0:T(8,128)} fusion(f32[128,32]{1,0:T(8,128)S(1)} %dynamic-slice_bitcast_fusion.6, bf16[2,128,32,128]{3,2,1,0:T(8,128)(2,1)S(1)} %get-tuple-element.234, s32[]{:T(128)} %get-tuple-element.220), kind=kOutput, calls=%fused_computation.10.clone.1 | convolution fusion | flops 135790592 | bytes 10503168 | tf_op jit(solution)/shard_map/while/body/eval_jaxpr/tsri,tsrj->tsij/dot_general | solution.py:76
  113.8 12.5 %convolution_add_fusion.4 = f32[8,16384]{1,0:T(8,128)S(1)} fusion(f32[16,8,128,128]{3,2,1,0:T(8,128)} %bitcast.121, f32[8,16384]{1,0:T(8,128)S(1)} %get-tuple-element.221, pred[]{:T(512)S(6)} %compare.15, f32[2,8,128]{2,1,0:T(8,128)S(1)} %get-tuple-element.232, s32[]{:T(128)} %get-tuple-element.220), kind=kOutput, calls=%fused_computation.6.clone.1 | convolution fusion | flops 201588736 | bytes 9441285 | tf_op jit(solution)/shard_map/while/body/eval_jaxpr/dot_general | solution.py:87
  126.4 0.9 fusion.50
  127.3 0.2 convolution_add_fusion.5
  127.5 5.2 %fusion.49 = f32[128,128,128]{2,1,0:T(8,128)} fusion(f32[128,32]{1,0:T(8,128)S(1)} %dynamic-slice_bitcast_fusion.6, bf16[2,128,32,128]{3,2,1,0:T(8,128)(2,1)S(1)} %get-tuple-element.234, s32[]{:T(128)} %get-tuple-element.220), kind=kOutput, calls=%fused_computation.10.clone.1 | convolution fusion | flops 135790592 | bytes 10503168 | tf_op jit(solution)/shard_map/while/body/eval_jaxpr/tsri,tsrj->tsij/dot_general | solution.py:76
  132.7 12.5 %convolution_add_fusion.4 = f32[8,16384]{1,0:T(8,128)S(1)} fusion(f32[16,8,128,128]{3,2,1,0:T(8,128)} %bitcast.121, f32[8,16384]{1,0:T(8,128)S(1)} %get-tuple-element.221, pred[]{:T(512)S(6)} %compare.15, f32[2,8,128]{2,1,0:T(8,128)S(1)} %get-tuple-element.232, s32[]{:T(128)} %get-tuple-element.220), kind=kOutput, calls=%fused_computation.6.clone.1 | convolution fusion | flops 201588736 | bytes 9441285 | tf_op jit(solution)/shard_map/while/body/eval_jaxpr/dot_general | solution.py:87
  145.2 0.9 fusion.50
  146.2 0.2 convolution_add_fusion.5
  146.3 114.8 %all-reduce.6.cloned.1.call-done = f32[128,128]{1,0:T(8,128)} async-done(((f32[128,128]{1,0:T(8,128)}), f32[128,128]{1,0:T(8,128)}) %all-reduce.6.cloned.1.call-update) | async-done | bytes 65552 | tf_op jit(solution)/shard_map/psum | solution.py:103
  261.2 0.1 copy.52
  261.3 0.1 copy.50
  261.4 0.9 and_select_fusion
  262.3 6.0 %all-to-all-start.1 = ((f32[128,2,32]{2,1,0:T(2,128)}), f32[128,2,32]{2,1,0:T(2,128)S(1)}, u32[]{:S(2)}, u32[]{:S(2)}) async-start(f32[128,2,32]{2,1,0:T(2,128)} %and_select_fusion), calls=%async_computation.1 | async-start | bytes 262144 | tf_op jit(solution)/shard_map/all_to_all | solution.py:124
  268.3 1.3 dynamic-slice
  270.2 8.9 %all-reduce.1 = f32[8,128]{1,0:T(8,128)S(1)} all-reduce(f32[8,128]{1,0:T(8,128)S(1)} %get-tuple-element.68), channel_id=3, replica_groups=mesh['ent'=128,'rep'=4] {'rep'}, use_global_device_ids=true, to_apply=%region_7.8.clone | all-reduce | flops 1024 | bytes 8192
  279.1 29.6 %all-reduce.8.cloned.1.call-done = (f32[8,16384]{1,0:T(8,128)}, f32[128,128]{1,0:T(8,128)}) async-done(((f32[8,16384]{1,0:T(8,128)}, f32[128,128]{1,0:T(8,128)}), (f32[8,16384]{1,0:T(8,128)}, f32[128,128]{1,0:T(8,128)})) %all-reduce.8.cloned.1.call-update) | async-done | bytes 589840
  308.7 1.1 dynamic-slice_bitcast_fusion.2
  309.9 0.9 convert_add_fusion
  311.0 23.5 %custom-call.9 = f32[2,128,128]{2,1,0:T(8,128)S(1)} custom-call(f32[2,128,128]{2,1,0:T(8,128)S(1)} %fusion.20), custom_call_target="Cholesky" | custom-call | tf_op jit(solution)/shard_map/jit(cholesky)/cholesky | solution.py:13
  334.5 0.1 compare_reduce_fusion
  334.7 19.7 %custom-call.10 = f32[2,1,128,128]{2,3,1,0:T(8,128)S(1)} custom-call(f32[2,1,128,128]{3,2,1,0:T(8,128)S(1)} %select_bitcast_fusion), custom_call_target="InvertDiagBlocksLowerTriangular" | custom-call | tf_op jit(solution)/shard_map/triangular_solve | solution.py:15
  354.4 0.2 convolution_bitcast_fusion
  354.6 0.3 fusion.17
  354.9 6.8 %all-gather = bf16[4,2,128]{2,1,0:T(2,128)(2,1)S(1)} all-gather(bf16[1,2,128]{2,1,0:T(2,128)(2,1)S(1)} %convert_bitcast_fusion), channel_id=1, replica_groups=mesh['ent'=128,'rep'=4] {'rep'}, dimensions={0}, use_global_device_ids=true | all-gather | bytes 2560 | tf_op jit(solution)/shard_map/all_gather | solution.py:109
  361.8 0.2 fusion.22
  362.0 30.6 %all_to_all.15 = f32[128,2,128]{2,1,0:T(2,128)S(1)} all-to-all(f32[128,2,128]{2,1,0:T(2,128)S(1)} %bitcast.132), channel_id=1, replica_groups=mesh['ent'=128,'rep'=4] {'ent'}, dimensions={0} | all-to-all | bytes 262144 | tf_op jit(solution)/shard_map/all_to_all | solution.py:117
  392.6 46.8 %while.23 = (s32[]{:T(128)}, f32[1024,128]{1,0:T(8,128)S(1)}, s32[2,128,32]{2,1,0:T(8,128)S(1)}, f32[2,128,1,32]{3,1,2,0:T(8,128)S(1)}, f32[2,128,1,128]{3,1,2,0:T(8,128)S(1)}, /*index=5*/s32[]{:T(128)}) while((s32[]{:T(128)}, f32[1024,128]{1,0:T(8,128)S(1)}, s32[2,128,32]{2,1,0:T(8,128)S(1)}, f32[2,128,1,32]{3,1,2,0:T(8,128)S(1)}, ...), condition=%wide.region_10.11_spmd, body=%wide.region_8.10_spmd.sunk | while | flops 1048578 | bytes 8749137 | solution.py:146
  392.8 0.6 bitcast_multiply_fusion.2
  393.5 22.6 %scatter_fusion = f32[1024,128]{1,0:T(8,128)S(1)} fusion(f32[1024,128]{1,0:T(8,128)S(1)} %get-tuple-element.245, s32[4096]{0:T(1024)S(1)} %reshape.259, f32[4096,128]{1,0:T(8,128)S(1)} %bitcast_multiply_fusion.2), kind=kCustom, calls=%fused_computation.1.clone.1 | custom fusion | flops 524288 | bytes 6307840 | tf_op jit(solution)/shard_map/while/body/eval_jaxpr/scatter-add | solution.py:137
  416.2 0.6 bitcast_multiply_fusion.2
  416.9 22.6 %scatter_fusion = f32[1024,128]{1,0:T(8,128)S(1)} fusion(f32[1024,128]{1,0:T(8,128)S(1)} %get-tuple-element.245, s32[4096]{0:T(1024)S(1)} %reshape.259, f32[4096,128]{1,0:T(8,128)S(1)} %bitcast_multiply_fusion.2), kind=kCustom, calls=%fused_computation.1.clone.1 | custom fusion | flops 524288 | bytes 6307840 | tf_op jit(solution)/shard_map/while/body/eval_jaxpr/scatter-add | solution.py:137
  439.5 0.8 broadcast_multiply_fusion
  (59 shorter events, 1.6 us)
Async XLA Ops:
  7.2 2.0 copy-start
  37.8 20.1 %copy-start.5 = (s32[1,1,128]{2,1,0:T(1,128)S(1)}, s32[1,1,128]{2,1,0:T(1,128)}, u32[]{:S(2)}) copy-start(s32[1,1,128]{2,1,0:T(1,128)} %param.15) | copy-start | bytes 1540
  37.8 21.1 %copy-start.2 = (s32[1,1,256,32]{2,3,1,0:T(8,128)S(1)}, s32[1,1,256,32]{2,3,1,0:T(8,128)}, u32[]{:S(2)}) copy-start(s32[1,1,256,32]{2,3,1,0:T(8,128)} %param.14) | copy-start | bytes 98308
  37.8 21.4 %copy-start.3 = (s32[1,1,256,1]{2,3,1,0:T(1,128)S(1)}, s32[1,1,256,1]{2,3,1,0:T(1,128)}, u32[]{:S(2)}) copy-start(s32[1,1,256,1]{2,3,1,0:T(1,128)} %param.13) | copy-start | bytes 3076
  37.8 70.8 %all-to-all-start = ((bf16[128,64,128]{2,1,0:T(8,128)(2,1)}), bf16[128,64,128]{2,1,0:T(8,128)(2,1)S(1)}, u32[]{:S(2)}, u32[]{:S(2)}) async-start(bf16[128,64,128]{2,1,0:T(8,128)(2,1)} %select_select_fusion), calls=%async_computation | async-start | bytes 4194304 | tf_op jit(solution)/shard_map/all_to_all | solution.py:43
  56.4 204.7 %all-reduce.6.cloned.1.call-start = ((), (), s32[]{:S(2)}) async-start(), calls=%async_computation.3 | async-start | bytes 131072 | tf_op jit(solution)/shard_map/psum | solution.py:103
  57.3 251.4 %all-reduce.8.cloned.1.call-start = ((), (), s32[]{:S(2)}) async-start(), calls=%async_computation.4 | async-start | bytes 1179648
  146.3 114.8 %copy-start.1 = (f32[8,16384]{1,0:T(8,128)}, f32[8,16384]{1,0:T(8,128)S(1)}, u32[]{:S(2)}) copy-start(f32[8,16384]{1,0:T(8,128)S(1)} %get-tuple-element.67) | copy-start | bytes 1572868
  262.3 99.7 %all-to-all-start.1 = ((f32[128,2,32]{2,1,0:T(2,128)}), f32[128,2,32]{2,1,0:T(2,128)S(1)}, u32[]{:S(2)}, u32[]{:S(2)}) async-start(f32[128,2,32]{2,1,0:T(2,128)} %and_select_fusion), calls=%async_computation.1 | async-start | bytes 262144 | tf_op jit(solution)/shard_map/all_to_all | solution.py:124
  354.9 37.7 %copy-start.4 = (f32[2,1,128]{2,1,0:T(1,128)}, f32[2,1,128]{2,1,0:T(1,128)S(1)}, u32[]{:S(2)}) copy-start(f32[2,1,128]{2,1,0:T(1,128)S(1)} %fusion.17) | copy-start | bytes 3076
Sparse Core Ops, SparseCore 0:
  60.5 200.5 all-reduce.5
  264.0 44.6 all-reduce.7
